TPU v7x, 256 devices: a whole 4x4x8 slice. The times are simulated.
256 devices in a mesh: ctx: 64 (over z, x, core), head: 4 (over y).
Axes of the slice: x: 4, y: 4, z: 8, core: 2. Of those that a mesh axis runs over, the one named last changes fastest.
Arguments:
- queries: float32 [16384, 4096], P('ctx', 'head'), may hold values from -48 to 48
- keys: float32 [16384, 4096], P('ctx', 'head'), may hold values from -48 to 48
- values: float32 [16384, 4096], P('ctx', 'head'), may hold values from -8 to 8
- query_map: float32 [32, 128, 128], P('head'), may hold values from -2 to 2
- key_map: float32 [32, 128, 128], P('head'), may hold values from -2 to 2
- out_weight: float32 [4096, 4096], P(None, ('ctx', 'head')), may hold values from -0.09375 to 0.09375
- residual: float32 [16384, 4096], P('ctx', 'head'), may hold values from -1.5 to 1.5
Outputs:
- layer_out: float32 [16384, 4096], P('ctx', 'head')
All inputs are finite; a program needn't handle non-finite values.
Results may differ from a plain program's by a relative error of at most 0.0001.
Values sent between devices are 32-bit elements; how exact they have to be, the bound alone decides.
A program may use at most 192 MiB of HBM per device.

v0:
```python
import jax
import jax.numpy as jnp
from jax import lax
from jax.sharding import PartitionSpec as P

HIGH = lax.Precision.HIGHEST


def carried_in(part, axis, combine, identity):
    place = lax.axis_index(axis)
    gathered = jax.tree.map(lambda a: lax.all_gather(a, axis), part)
    state = jax.tree.map(lambda a, e: jnp.zeros_like(a) + jnp.asarray(e, a.dtype), part, identity)

    def one(step, state):
        return combine(
            state, jax.tree.map(lambda a: lax.dynamic_index_in_dim(a, step, 0, False), gathered)
        )

    return lax.fori_loop(0, place, one, state)


def feature_map(inputs, weights):
    scores = jnp.einsum("nhd,hdf->hnf", inputs, weights, precision=HIGH)
    return jnp.concatenate(
        [jax.nn.softmax(scores, axis=-1), jax.nn.softmax(-scores, axis=-1)], axis=-1
    )


def add_pair(earlier, later):
    return (earlier[0] + later[0], earlier[1] + later[1])


def body(queries, keys, values, query_map, key_map, out_weight, residual):
    rows = queries.shape[0]
    heads_here, head_size, _ = query_map.shape
    width = heads_here * head_size
    shaped = (rows, heads_here, head_size)
    query_feat = feature_map(queries.reshape(shaped), query_map)
    key_feat = feature_map(keys.reshape(shaped), key_map)
    value_heads = values.reshape(shaped).transpose(1, 0, 2)
    local_state = jnp.einsum("hkf,hkd->hfd", key_feat, value_heads, precision=HIGH)
    local_norm = jnp.sum(key_feat, axis=1)
    zero_pair = (jnp.zeros_like(local_state), jnp.zeros_like(local_norm))
    prior_state, prior_norm = carried_in((local_state, local_norm), "ctx", add_pair, zero_pair)
    causal = jnp.tril(jnp.ones((rows, rows), jnp.float32))
    weights = jnp.einsum("hqf,hkf->hqk", query_feat, key_feat, precision=HIGH) * causal
    numer = jnp.einsum("hqk,hkd->hqd", weights, value_heads, precision=HIGH)
    numer = numer + jnp.einsum("hqf,hfd->hqd", query_feat, prior_state, precision=HIGH)
    denom = jnp.sum(weights, axis=-1) + jnp.einsum(
        "hqf,hf->hq", query_feat, prior_norm, precision=HIGH
    )
    mixed = (numer / denom[..., None]).transpose(1, 0, 2).reshape(rows, width)
    own_rows = lax.all_to_all(out_weight, "head", split_axis=0, concat_axis=1, tiled=True)
    partial_value = jnp.dot(
        mixed,
        lax.all_gather(own_rows, "ctx", axis=1, tiled=True),
        precision=HIGH,
        preferred_element_type=jnp.float32,
    )
    projected = lax.psum_scatter(partial_value, "head", scatter_dimension=1, tiled=True)
    return residual + projected


def solution(mesh):
    placed = (
        P("ctx", "head"),
        P("ctx", "head"),
        P("ctx", "head"),
        P("head", None, None),
        P("head", None, None),
        P(None, ("ctx", "head")),
        P("ctx", "head"),
    )
    return jax.shard_map(
        body, mesh=mesh, in_specs=placed, out_specs=P("ctx", "head"), check_vma=False
    )
```

profile of v0, /device:TPU:1, one launch (start us, length us, event | category | flops | bytes accessed | tf_op | source)
XLA Modules:
  0.0 486.4 jit_solution(5535288748645154746)
XLA Ops:
  6.5 0.0 copy-start
  6.5 0.0 all-gather.7.cloned.1.call-start
  6.5 1.2 copy-done
  7.8 2.1 fusion.29
  9.9 1.1 fusion.46
  11.0 1.1 fusion.47
  12.1 0.0 copy-start.6
  12.1 0.2 broadcast_divide_fusion
  12.3 0.0 copy-start.3
  12.3 1.3 copy-done.6
  13.6 3.0 fusion.24
  16.6 0.0 all-gather.7.cloned.1.call-update
  16.6 0.0 all-gather.5.cloned.1.call-start
  16.6 0.0 copy-done.11
  16.7 10.4 %all_to_all.19 = f32[4,1024,16]{1,2,0:T(8,128)} all-to-all(f32[4,1024,16]{1,2,0:T(8,128)S(1)} %bitcast.68), channel_id=1, replica_groups=mesh['ctx'=64,'head'=4] {'head'}, dimensions={0} | all-to-all | bytes 524288 | tf_op jit(solution)/shard_map/all_to_all | solution.py:53
  27.1 0.0 all-gather.5.cloned.1.call-update
  27.1 0.0 reduce-scatter.2.cloned.1.call-start
  27.2 0.0 copy-start.9
  27.2 0.0 copy-start.10
  27.2 2.5 copy.70
  29.8 0.0 copy-done.3
  29.8 0.3 fusion.23
  30.1 60.9 %all-gather.1 = f32[512,256]{1,0:T(8,128)} all-gather(f32[8,256]{1,0:T(8,128)S(1)} %fusion.23), channel_id=3, replica_groups=mesh['ctx'=64,'head'=4] {'ctx'}, dimensions={0}, use_global_device_ids=true | all-gather | bytes 532480 | tf_op jit(solution)/shard_map/all_gather | solution.py:11
  91.1 0.0 copy-done.9
  91.1 0.0 copy-done.10
  91.1 1.1 fusion.32
  92.2 1.1 fusion.48
  93.3 1.1 fusion.49
  94.4 0.0 copy-start.4
  94.4 0.2 broadcast_divide_fusion.2
  94.6 0.0 copy-start.1
  94.6 1.0 copy-done.1
  95.6 0.3 copy-done.4
  96.0 4.8 multiply_reduce_fusion
  100.8 157.3 %all-gather.7.cloned.1.call-done = f32[512,256,128]{2,1,0:T(8,128)} async-done(((f32[8,256,128]{2,1,0:T(8,128)}), f32[512,256,128]{2,1,0:T(8,128)}) %all-gather.7.cloned.1.call-update) | async-done | bytes 67108880 | tf_op jit(solution)/shard_map/all_gather | solution.py:11
  258.1 0.1 broadcast_in_dim.11
  258.2 2.4 while.12
  258.4 1.5 bitcast_add_fusion.5
  259.9 0.7 bitcast_add_fusion.6
  260.6 2.5 fusion.26
  263.1 0.0 copy-start.7
  263.1 2.0 fusion.27
  265.2 2.2 fusion.20
  267.4 89.8 %all-gather.5.cloned.1.call-done = f32[1024,4096]{0,1:T(8,128)} async-done(((f32[1024,64]{0,1:T(8,128)}), f32[1024,4096]{0,1:T(8,128)}) %all-gather.5.cloned.1.call-update) | async-done | bytes 16777232 | tf_op jit(solution)/shard_map/all_gather | solution.py:56
  357.2 30.4 %fusion.50 = f32[256,4096]{1,0:T(8,128)} fusion(f32[256,1024]{0,1:T(8,128)S(1)} %bitcast.64, f32[1024,4096]{0,1:T(8,128)} %all-gather.5.cloned.1.call-done), kind=kOutput, calls=%fused_computation.59 | convolution fusion | flops 12884901888 | bytes 22020096 | tf_op jit(solution)/shard_map/dot_general | solution.py:54
  387.6 0.0 reduce-scatter.2.cloned.1.call-update
  387.6 89.9 %reduce-scatter.2.cloned.1.call-done = f32[256,1024]{1,0:T(8,128)} async-done(((f32[256,4096]{1,0:T(8,128)}), f32[256,1024]{1,0:T(8,128)}) %reduce-scatter.2.cloned.1.call-update) | async-done | bytes 1048592 | tf_op jit(solution)/shard_map/reduce_scatter | solution.py:60
  477.6 2.3 add.38
  (12 shorter events, 0.1 us)
Async XLA Ops:
  6.5 1.2 copy-start
  6.5 251.6 %all-gather.7.cloned.1.call-start = ((), (), s32[]{:S(2)}) async-start(), calls=%async_computation.4 | async-start | bytes 68157440 | tf_op jit(solution)/shard_map/all_gather | solution.py:11
  12.1 1.5 copy-start.6
  12.3 17.4 %copy-start.3 = (f32[8,256,128]{1,2,0:T(8,128)}, f32[8,256,128]{1,2,0:T(8,128)S(1)}, u32[]{:S(2)}) copy-start(f32[8,256,128]{1,2,0:T(8,128)S(1)} %get-tuple-element.64) | copy-start | bytes 3145732
  13.6 3.0 copy-start.11
  16.6 340.6 %all-gather.5.cloned.1.call-start = ((), (), s32[]{:S(2)}) async-start(), calls=%async_computation.2 | async-start | bytes 17039360 | tf_op jit(solution)/shard_map/all_gather | solution.py:56
  27.1 450.4 %reduce-scatter.2.cloned.1.call-start = ((), (), s32[]{:S(2)}) async-start(), calls=%async_computation.3 | async-start | bytes 5242880 | tf_op jit(solution)/shard_map/reduce_scatter | solution.py:60
  27.2 63.9 %copy-start.9 = (f32[256,1024]{1,0:T(8,128)S(1)}, f32[256,1024]{1,0:T(8,128)}, u32[]{:S(2)}) copy-start(f32[256,1024]{1,0:T(8,128)} %param.9) | copy-start | bytes 3145732
  27.2 63.9 %copy-start.10 = (f32[8,128,128]{2,1,0:T(8,128)S(1)}, f32[8,128,128]{2,1,0:T(8,128)}, u32[]{:S(2)}) copy-start(f32[8,128,128]{2,1,0:T(8,128)} %param.12) | copy-start | bytes 1572868
  94.4 1.5 copy-start.4
  94.6 1.0 copy-start.1
  260.6 2.5 copy-start.2
  263.1 2.0 copy-start.5
  263.1 2.0 copy-start.7
  387.6 90.0 %copy-start.8 = (f32[256,1024]{1,0:T(8,128)S(1)}, f32[256,1024]{1,0:T(8,128)}, u32[]{:S(2)}) copy-start(f32[256,1024]{1,0:T(8,128)} %param.15) | copy-start | bytes 3145732
Sparse Core Ops, SparseCore 0:
  16.7 241.3 all-gather.6
  260.9 96.2 all-gather.4
  387.7 89.7 reduce-scatter.1
where the time goes:
time: 492 us; the launch traced here: 486 us
  waiting for transfers between devices  337 us (68%)
  blocking collectives  71.4 us (15%)
  matrix products  48.2 us (10%)
  between operations  13.3 us (3%)
  other arithmetic  9.65 us (2%)
  local copies, waits for them, and re-layouts  6.49 us (1%)
    all_gather x1, waiting for transfers between devices, carried_in(): gathered = jax.tree.map(lambda a: lax.all_gather(a, axis), part)  157 us
    reduce_scatter x1, waiting for transfers between devices, body(): lax.psum_scatter(partial_value, 'head', scatter_dimension=1, tiled=True)  89.9 us
    all_gather x1, waiting for transfers between devices, body(): lax.all_gather(own_rows, 'ctx', axis=1, tiled=True)  89.8 us
    all_gather x1, blocking collectives, carried_in(): gathered = jax.tree.map(lambda a: lax.all_gather(a, axis), part)  60.9 us
    dot_general x1, matrix products, body(): jnp.dot(mixed, lax.all_gather(own_rows, 'ctx', axis=1, tiled=True), preci...  30.4 us
    all_to_all x1, blocking collectives, body(): lax.all_to_all(out_weight, 'head', split_axis=0, concat_axis=1, tiled=True)  10.4 us
  transfers between devices with their start and end apart: 3, of which 3 were waited for; matrix products, arithmetic and copies ran while one was open for 4% of the time, Pallas kernels for 0%

commit v1 on v0

--- a/solution.py
+++ b/solution.py
@@ -4,6 +4,13 @@
 from jax.sharding import PartitionSpec as P
 
 HIGH = lax.Precision.HIGHEST
+
+
+def swapped_in(array, axis, dim):
+    size = lax.axis_size(axis)
+    blocks = jnp.stack([array for _ in range(size)])
+    blocks = lax.all_to_all(blocks, axis, split_axis=0, concat_axis=0)
+    return jnp.concatenate(blocks, axis=dim)
 
 
 def carried_in(part, axis, combine, identity):
@@ -52,10 +59,7 @@
     mixed = (numer / denom[..., None]).transpose(1, 0, 2).reshape(rows, width)
     own_rows = lax.all_to_all(out_weight, "head", split_axis=0, concat_axis=1, tiled=True)
     partial_value = jnp.dot(
-        mixed,
-        lax.all_gather(own_rows, "ctx", axis=1, tiled=True),
-        precision=HIGH,
-        preferred_element_type=jnp.float32,
+        mixed, swapped_in(own_rows, "ctx", 1), precision=HIGH, preferred_element_type=jnp.float32
     )
     projected = lax.psum_scatter(partial_value, "head", scatter_dimension=1, tiled=True)
     return residual + projected

time: 492 us -> 869 us (1.77)
  blocking collectives: 71.4 us -> 583 us
  waiting for transfers between devices: 337 us -> 180 us
  starting transfers between devices: 0.09 us -> 13.7 us
  local copies, waits for them, and re-layouts: 6.49 us -> 15.2 us
    all_gather x1, blocking collectives: 60.9 us -> 572 us  [carried_in(): gathered = jax.tree.map(lambda a: lax.all_gather(a, axis), part)]
    all_gather x1, waiting for transfers between devices: 157 us -> 0.01 us  [carried_in(): gathered = jax.tree.map(lambda a: lax.all_gather(a, axis), part)]
    reduce_scatter x1, waiting for transfers between devices: 89.9 us -> 180 us  [body(): lax.psum_scatter(partial_value, 'head', scatter_dimension=1, tiled=True)]
    all_gather x1 -> x0, waiting for transfers between devices: 89.8 us -> none  [body(): lax.all_gather(own_rows, 'ctx', axis=1, tiled=True)]
    all_to_all x0 -> x1, starting transfers between devices: none -> 13.6 us  [swapped_in(): blocks = lax.all_to_all(blocks, axis, split_axis=0, concat_axis=0)]
    another operation x0 -> x1, local copies, waits for them, and re-layouts: none -> 8.76 us  [swapped_in(): blocks = jnp.stack([array for _ in range(size)])]
  transfers between devices with their start and end apart: 3 -> 3, of which waited for: 3 -> 1; matrix products, arithmetic and copies ran while one was open for 4% -> 3% of each run, Pallas kernels for 0% -> 0%
where the time goes in v1:
time: 869 us; the launch traced here: 863 us
  blocking collectives  583 us (67%)
  waiting for transfers between devices  180 us (21%)
  matrix products  48.5 us (6%)
  local copies, waits for them, and re-layouts  15.2 us (2%)
  starting transfers between devices  13.7 us (2%)
  between operations  13.6 us (2%)
  other arithmetic  9.65 us (1%)
    all_gather x1, blocking collectives, carried_in(): gathered = jax.tree.map(lambda a: lax.all_gather(a, axis), part)  572 us
    reduce_scatter x1, waiting for transfers between devices, body(): lax.psum_scatter(partial_value, 'head', scatter_dimension=1, tiled=True)  180 us
    dot_general x1, matrix products, body(): jnp.dot(mixed, swapped_in(own_rows, 'ctx', 1), precision=HIGH, preferred_...  30.7 us
  transfers between devices with their start and end apart: 3, of which 1 were waited for; matrix products, arithmetic and copies ran while one was open for 3% of the time, Pallas kernels for 0%

profile of v1, /device:TPU:1, one launch (start us, length us, event | category | flops | bytes accessed | tf_op | source)
XLA Modules:
  0.0 863.0 jit_solution(18222511581191667597)
XLA Ops:
  6.5 0.0 copy-start
  6.5 0.0 all-gather.4.cloned.1.call-start
  6.5 1.2 copy-done
  7.8 2.1 fusion.29
  9.9 1.1 fusion.46
  11.0 1.1 fusion.47
  12.1 0.0 copy-start.6
  12.1 0.2 broadcast_divide_fusion
  12.3 0.0 copy-start.3
  12.3 1.3 copy-done.6
  13.6 3.0 fusion.24
  16.6 0.0 all-gather.4.cloned.1.call-update
  16.6 0.0 copy-done.11
  16.6 10.4 %all_to_all.21 = f32[4,1024,16]{1,2,0:T(8,128)S(1)} all-to-all(f32[4,1024,16]{1,2,0:T(8,128)S(1)} %bitcast.71), channel_id=1, replica_groups=mesh['ctx'=64,'head'=4] {'head'}, dimensions={0} | all-to-all | bytes 524288 | tf_op jit(solution)/shard_map/all_to_all | solution.py:60
  27.0 8.8 %stack.5 = f32[64,1024,64]{1,2,0:T(8,128)} broadcast(f32[1024,64]{0,1:T(8,128)S(1)} %bitcast.70), dimensions={1,2} | broadcast | bytes 17039360 | tf_op jit(solution)/shard_map/stack | solution.py:11
  35.7 13.6 %all-to-all-start.1 = ((f32[64,1024,64]{1,2,0:T(8,128)}), f32[64,1024,64]{1,2,0:T(8,128)}, u32[]{:S(2)}, u32[]{:S(2)}) async-start(f32[64,1024,64]{1,2,0:T(8,128)} %stack.5), calls=%async_computation.1 | async-start | bytes 33554432 | tf_op jit(solution)/shard_map/all_to_all | solution.py:12
  49.4 0.0 reduce-scatter.2.cloned.1.call-start
  49.4 0.0 copy-start.9
  49.4 0.0 copy-start.10
  49.5 2.5 copy.70
  52.0 0.0 copy-done.3
  52.0 0.3 fusion.23
  52.4 572.2 %all-gather.1 = f32[512,256]{1,0:T(8,128)} all-gather(f32[8,256]{1,0:T(8,128)S(1)} %fusion.23), channel_id=3, replica_groups=mesh['ctx'=64,'head'=4] {'ctx'}, dimensions={0}, use_global_device_ids=true | all-gather | bytes 532480 | tf_op jit(solution)/shard_map/all_gather | solution.py:18
  624.6 0.0 copy-done.9
  624.6 0.0 copy-done.10
  624.6 1.1 fusion.32
  625.8 1.1 fusion.48
  626.9 1.1 fusion.49
  628.0 0.0 copy-start.4
  628.0 0.2 broadcast_divide_fusion.2
  628.2 1.0 copy-done.1
  629.2 0.3 copy-done.4
  629.5 4.8 multiply_reduce_fusion
  634.3 0.1 broadcast_in_dim.11
  634.4 2.2 while.12
  634.4 1.5 bitcast_add_fusion.5
  635.9 0.7 bitcast_add_fusion.6
  636.6 2.5 fusion.26
  639.1 0.0 copy-done.2
  639.1 2.0 fusion.27
  641.1 0.0 copy-done.5
  641.2 0.0 copy-done.7
  641.2 2.2 fusion.20
  643.4 0.0 all-to-all-done.1
  643.4 30.7 %fusion.50 = f32[256,4096]{1,0:T(8,128)} fusion(f32[256,1024]{0,1:T(8,128)S(1)} %bitcast.67, f32[1024,4096]{0,1:T(8,128)} %bitcast.14), kind=kOutput, calls=%fused_computation.59 | convolution fusion | flops 12884901888 | bytes 22020096 | tf_op jit(solution)/shard_map/dot_general | solution.py:61
  674.1 0.0 reduce-scatter.2.cloned.1.call-update
  674.1 179.7 %reduce-scatter.2.cloned.1.call-done = f32[256,1024]{1,0:T(8,128)} async-done(((f32[256,4096]{1,0:T(8,128)}), f32[256,1024]{1,0:T(8,128)}) %reduce-scatter.2.cloned.1.call-update) | async-done | bytes 1048592 | tf_op jit(solution)/shard_map/reduce_scatter | solution.py:64
  853.9 2.3 add.38
  (12 shorter events, 0.1 us)
Async XLA Ops:
  6.5 1.2 copy-start
  6.5 627.8 %all-gather.4.cloned.1.call-start = ((), (), s32[]{:S(2)}) async-start(), calls=%async_computation.4 | async-start | bytes 68157440 | tf_op jit(solution)/shard_map/all_gather | solution.py:18
  12.1 1.5 copy-start.6
  12.3 39.7 %copy-start.3 = (f32[8,256,128]{1,2,0:T(8,128)}, f32[8,256,128]{1,2,0:T(8,128)S(1)}, u32[]{:S(2)}) copy-start(f32[8,256,128]{1,2,0:T(8,128)S(1)} %get-tuple-element.64) | copy-start | bytes 3145732
  13.6 3.0 copy-start.11
  35.7 607.6 %all-to-all-start.1 = ((f32[64,1024,64]{1,2,0:T(8,128)}), f32[64,1024,64]{1,2,0:T(8,128)}, u32[]{:S(2)}, u32[]{:S(2)}) async-start(f32[64,1024,64]{1,2,0:T(8,128)} %stack.5), calls=%async_computation.1 | async-start | bytes 33554432 | tf_op jit(solution)/shard_map/all_to_all | solution.py:12
  49.4 804.5 %reduce-scatter.2.cloned.1.call-start = ((), (), s32[]{:S(2)}) async-start(), calls=%async_computation.3 | async-start | bytes 5242880 | tf_op jit(solution)/shard_map/reduce_scatter | solution.py:64
  49.4 575.2 %copy-start.9 = (f32[256,1024]{1,0:T(8,128)S(1)}, f32[256,1024]{1,0:T(8,128)}, u32[]{:S(2)}) copy-start(f32[256,1024]{1,0:T(8,128)} %param.9) | copy-start | bytes 3145732
  49.4 575.2 %copy-start.10 = (f32[8,128,128]{2,1,0:T(8,128)S(1)}, f32[8,128,128]{2,1,0:T(8,128)}, u32[]{:S(2)}) copy-start(f32[8,128,128]{2,1,0:T(8,128)} %param.12) | copy-start | bytes 1572868
  628.0 1.5 copy-start.4
  628.2 1.0 copy-start.1
  636.6 2.5 copy-start.2
  639.1 2.0 copy-start.5
  639.1 2.0 copy-start.7
  674.1 179.8 %copy-start.8 = (f32[256,1024]{1,0:T(8,128)S(1)}, f32[256,1024]{1,0:T(8,128)}, u32[]{:S(2)}) copy-start(f32[256,1024]{1,0:T(8,128)} %param.15) | copy-start | bytes 3145732
Sparse Core Ops, SparseCore 0:
  16.7 583.3 all-gather.3
  674.3 179.5 reduce-scatter.1
